TPU v7x, 512 devices: a whole 4x4x16 slice. The times are simulated.
512 devices in a mesh: blk: 64 (over z, x), scale: 8 (over y, core).
Axes of the slice: x: 4, y: 4, z: 16, core: 2. Of those that a mesh axis runs over, the one named last changes fastest.
Arguments:
- start_block: float32 [64, 524288], P(None, ('blk', 'scale')), may hold values from -90 to 90
- blocks: bfloat16 [16384, 128, 128], P(('blk', 'scale')), may hold values from -0.1875 to 0.1875
- block_column: int32 [16384], P(('blk', 'scale')), may hold values from 0 to 7
- block_target: int32 [16384], P(('blk', 'scale')), may hold values from 0 to 15, as said below
- block_count: int32 [512], P(('blk', 'scale')), may hold values from 2 to 32, as said below
- partner: int32 [524288], P(('blk', 'scale')), may hold values from 0 to 1023, as said below
- degree: int32 [524288], P(('blk', 'scale')), may hold values from 1 to 16
Outputs:
- subspace: float32 [64, 524288], P(None, ('blk', 'scale'))
- rayleigh: float32 [64, 64], replicated
Inputs may be any that keep to these rules, and one draw needn't show every extreme that they name: block_count[g] is the number of live slots of row group g; it is at least 2; some row group has all 32 slots live in every draw. In each row group, slots c < 2 have block_target of 8 or more, and all other slots have block_target below 8. Within each row group, partner is a permutation of 0 to 1023, and the pairing is mutual: if node i of group (b, s) has partner j, then node j of group (b, s xor 1) has partner i.
All inputs are finite; a program needn't handle non-finite values.
Results may differ from a plain program's by a relative error of at most 0.0011.
Values may be sent and summed in bfloat16 or wider, within the bound.
No kernel may reach another device: no remote copies, remote signals or barrier semaphores. Data moves between devices by JAX's collectives and lax.ppermute only.
A program may use at most 64 MiB of HBM per device.

v0:
```python
import jax
import jax.numpy as jnp
from jax import lax
from jax.sharding import PartitionSpec as P

ITERS = 2
FULL_PRECISION = lax.Precision.HIGHEST


def from_behind(block, axis, distance):
    devices = range(lax.axis_size(axis))
    route = [((i - distance) % len(devices), i) for i in devices]
    return lax.ppermute(block, axis, route)


def swapped(array, axis, apart):
    return lax.ppermute(array, axis, [(i, i ^ 1 << apart) for i in range(lax.axis_size(axis))])


def pick_rows(onehot, source):
    picked = jnp.einsum(
        "cr,krj->ckj", onehot.astype(jnp.bfloat16), source, preferred_element_type=jnp.float32
    )
    return picked.astype(jnp.bfloat16)


def place_rows(onehot, partial_terms):
    return jnp.einsum("cr,ckj->krj", onehot, partial_terms, precision=FULL_PRECISION)


def slot_masks(columns, targets, slot_count, row_blocks):
    live_mask = (jnp.arange(columns.shape[0]) < slot_count[0]).astype(jnp.float32)[:, None]
    onecol = (columns[:, None] == jnp.arange(row_blocks)[None, :]).astype(jnp.float32) * live_mask
    onetgt = (targets[:, None] == jnp.arange(2 * row_blocks)[None, :]).astype(
        jnp.float32
    ) * live_mask
    return (onecol, onetgt)


def forward_terms(source, weights, onecol):
    picked = pick_rows(onecol, source)
    return jnp.einsum("cki,cji->ckj", picked, weights, preferred_element_type=jnp.float32)


def backward_terms(stacked, weights, onetgt):
    picked = pick_rows(onetgt, stacked)
    return jnp.einsum("ckj,cji->cki", picked, weights, preferred_element_type=jnp.float32)


def over_slots(term_fn, slot_total, initial):
    return jax.tree.map(jnp.add, initial, term_fn(0, slot_total))


def apply_operator(
    vectors, inv_sqrt_degree, blocks, block_column, block_target, block_count, partner
):
    vector_count, node_rows = vectors.shape
    row_blocks = node_rows // 128
    scaled = (vectors * inv_sqrt_degree[None, :]).astype(jnp.bfloat16)
    own_vectors = scaled.reshape(vector_count, row_blocks, 128)
    next_vectors = from_behind(own_vectors, "blk", -1)
    stacked = jnp.concatenate([own_vectors, next_vectors], axis=1)
    onecol, onetgt = slot_masks(block_column, block_target, block_count, row_blocks)
    empty_sum = jnp.zeros((vector_count, row_blocks, 128), jnp.float32)

    def local_terms(first_slot, slot_width):
        forward = forward_terms(own_vectors, blocks, onecol)
        backward = backward_terms(stacked, blocks, onetgt)
        nearby = place_rows(onetgt[:, :row_blocks], forward) + place_rows(onecol, backward)
        return (nearby, place_rows(onetgt[:, row_blocks:], forward))

    nearby, ahead_sum = over_slots(local_terms, blocks.shape[0], (empty_sum, empty_sum))
    surface = nearby + from_behind(ahead_sum.astype(jnp.bfloat16), "blk", 1).astype(ahead_sum.dtype)
    partner_vectors = swapped(scaled, "scale", 0)
    crossed = jnp.take(partner_vectors, partner, axis=1).astype(jnp.float32)
    return vectors + inv_sqrt_degree[None, :] * (surface.reshape(vector_count, node_rows) + crossed)


def shards(start_block, blocks, block_column, block_target, block_count, partner, degree):
    inv_sqrt_degree = 1.0 / jnp.sqrt(degree.astype(jnp.float32))
    vector_count = start_block.shape[0]
    node_total = start_block.shape[1] * lax.axis_size("blk") * lax.axis_size("scale")

    def operate(vectors):
        return apply_operator(
            vectors, inv_sqrt_degree, blocks, block_column, block_target, block_count, partner
        )

    subspace = start_block
    for sweep_index in range(ITERS):
        orthonormal_images = operate(subspace)
        local_gram = jnp.dot(orthonormal_images, orthonormal_images.T, precision=FULL_PRECISION)
        gram_matrix = lax.psum(local_gram, ("blk", "scale")) / node_total
        factor = jnp.linalg.cholesky(gram_matrix)
        factor_inverse = jax.scipy.linalg.solve_triangular(
            factor, jnp.eye(vector_count, dtype=jnp.float32), lower=True
        )
        subspace = jnp.dot(factor_inverse, orthonormal_images, precision=FULL_PRECISION)
    images = operate(subspace)
    local_projection = jnp.dot(subspace, images.T, precision=FULL_PRECISION)
    rayleigh = lax.psum(local_projection, ("blk", "scale")) / node_total
    return (subspace, rayleigh)


def solution(mesh):
    return jax.shard_map(
        shards,
        mesh=mesh,
        in_specs=(
            P(None, ("blk", "scale")),
            P(("blk", "scale"), None, None),
            P(("blk", "scale")),
            P(("blk", "scale")),
            P(("blk", "scale")),
            P(("blk", "scale")),
            P(("blk", "scale")),
        ),
        out_specs=(P(None, ("blk", "scale")), P()),
        check_vma=False,
    )
```

profile of v0, /device:TPU:1, one launch (start us, length us, event | category | flops | bytes accessed | tf_op | source)
XLA Modules:
  0.0 408.4 jit_solution(9733213956229735695)
XLA Ops:
  2.4 14.1 %collective-permute-start = (bf16[64,8,128]{2,1,0:T(8,128)(2,1)S(1)}, bf16[64,8,128]{2,1,0:T(8,128)(2,1)S(1)}, u32[]{:S(2)}, u32[]{:S(2)}) collective-permute-start(bf16[64,8,128]{2,1,0:T(8,128)(2,1)S(1)} %bitcast.141), channel_id=1, source_target_pairs={{8,0},{16,8},{24,16},{32,24},{40,32},{48,40},{56,48},{64,56},{72,6... | collective-permute-start | bytes 393224 | tf_op jit(solution)/shard_map/ppermute | solution.py:13
  19.4 1.2 fusion.3
  20.6 1.9 collective-permute-start.1
  22.6 2.9 collective-permute-start.2
  28.2 3.2 gather_fusion
  31.6 1.9 convert_add_fusion.2
  34.6 103.9 %psum.21 = f32[64,64]{0,1:T(8,128)S(1)} all-reduce(f32[64,64]{0,1:T(8,128)S(1)} %fusion.118), channel_id=1, replica_groups=mesh['blk'=64,'scale'=8] {'blk','scale'}, use_global_device_ids=true, to_apply=%region_0.0 | all-reduce | flops 4096 | bytes 32768 | tf_op jit(solution)/shard_map/psum | solution.py:93
  138.7 5.8 %cholesky.44 = f32[64,64]{1,0:T(8,128)S(1)} custom-call(f32[64,64]{1,0:T(8,128)S(1)} %fusion.60), custom_call_target="Cholesky" | custom-call | tf_op jit(solution)/shard_map/jit(cholesky)/cholesky | solution.py:94
  145.9 4.9 %custom-call.6 = f32[1,64,64]{1,2,0:T(8,128)S(1)} custom-call(f32[1,64,64]{2,1,0:T(8,128)S(1)} %fusion.55), custom_call_target="InvertDiagBlocksLowerTriangular" | custom-call | tf_op jit(solution)/shard_map/jit(_solve_triangular)/triangular_solve | solution.py:95
  152.5 1.9 collective-permute-start.3
  154.4 2.9 collective-permute-start.5
  159.4 3.8 collective-permute-start.4
  165.4 3.2 gather_fusion.1
  169.6 1.9 convert_add_fusion.1
  172.7 99.6 %psum.22 = f32[64,64]{0,1:T(8,128)S(1)} all-reduce(f32[64,64]{0,1:T(8,128)S(1)} %fusion.122), channel_id=1, replica_groups=mesh['blk'=64,'scale'=8] {'blk','scale'}, use_global_device_ids=true, to_apply=%region_3.7 | all-reduce | flops 4096 | bytes 32768 | tf_op jit(solution)/shard_map/psum | solution.py:93
  272.4 5.8 %cholesky.55 = f32[64,64]{1,0:T(8,128)S(1)} custom-call(f32[64,64]{1,0:T(8,128)S(1)} %fusion.58), custom_call_target="Cholesky" | custom-call | tf_op jit(solution)/shard_map/jit(cholesky)/cholesky | solution.py:94
  279.6 4.9 %custom-call.7 = f32[1,64,64]{1,2,0:T(8,128)S(1)} custom-call(f32[1,64,64]{2,1,0:T(8,128)S(1)} %fusion.56), custom_call_target="InvertDiagBlocksLowerTriangular" | custom-call | tf_op jit(solution)/shard_map/jit(_solve_triangular)/triangular_solve | solution.py:95
  286.2 4.8 %collective-permute-start.6 = (bf16[64,8,128]{2,1,0:T(8,128)(2,1)S(1)}, bf16[64,8,128]{2,1,0:T(8,128)(2,1)S(1)}, u32[]{:S(2)}, u32[]{:S(2)}) collective-permute-start(bf16[64,8,128]{2,1,0:T(8,128)(2,1)S(1)} %bitcast.145), channel_id=1, source_target_pairs={{8,0},{16,8},{24,16},{32,24},{40,32},{48,40},{56,48},{64,56},{72,6... | collective-permute-start | bytes 393224 | tf_op jit(solution)/shard_map/ppermute | solution.py:13
  291.0 2.9 collective-permute-start.8
  294.7 1.3 fusion.5
  296.0 2.1 collective-permute-start.7
  300.3 3.2 gather_fusion.2
  303.7 2.6 collective-permute-done.7
  308.6 99.2 %psum.23 = f32[64,64]{0,1:T(8,128)S(1)} all-reduce(f32[64,64]{0,1:T(8,128)S(1)} %fusion.24), channel_id=1, replica_groups=mesh['blk'=64,'scale'=8] {'blk','scale'}, use_global_device_ids=true, to_apply=%region_4.8 | all-reduce | flops 4096 | bytes 32768 | tf_op jit(solution)/shard_map/psum | solution.py:101
  (98 shorter events, 26.6 us)
Async XLA Ops:
  0.6 17.9 %copy-start = (bf16[32,128,128]{2,1,0:T(8,128)(2,1)S(1)}, bf16[32,128,128]{2,1,0:T(8,128)(2,1)}, u32[]{:S(2)}) copy-start(bf16[32,128,128]{2,1,0:T(8,128)(2,1)} %param.13) | copy-start | bytes 3145732
  2.4 24.9 %collective-permute-start = (bf16[64,8,128]{2,1,0:T(8,128)(2,1)S(1)}, bf16[64,8,128]{2,1,0:T(8,128)(2,1)S(1)}, u32[]{:S(2)}, u32[]{:S(2)}) collective-permute-start(bf16[64,8,128]{2,1,0:T(8,128)(2,1)S(1)} %bitcast.141), channel_id=1, source_target_pairs={{8,0},{16,8},{24,16},{32,24},{40,32},{48,40},{56,48},{64,56},{72,6... | collective-permute-start | bytes 393224 | tf_op jit(solution)/shard_map/ppermute | solution.py:13
  17.9 9.5 %copy-start.3 = (f32[32]{0:T(128)}, f32[32]{0:T(128)S(1)}, u32[]{:S(2)}) copy-start(f32[32]{0:T(128)S(1)} %compare_convert_fusion) | copy-start | bytes 388
  19.4 3.2 copy-start.1
  20.6 11.0 %collective-permute-start.1 = (bf16[64,8,128]{2,1,0:T(8,128)(2,1)S(1)}, bf16[64,8,128]{2,1,0:T(8,128)(2,1)S(1)}, u32[]{:S(2)}, u32[]{:S(2)}) collective-permute-start(bf16[64,8,128]{2,1,0:T(8,128)(2,1)S(1)} %fusion.3), channel_id=1, source_target_pairs={{504,0},{0,8},{8,16},{16,24},{24,32},{32,40},{40,48},{48,56},{56,6... | collective-permute-start | bytes 393224 | tf_op jit(solution)/shard_map/ppermute | solution.py:13
  22.6 4.1 %copy-start.14 = (s32[1024]{0:T(1024)S(1)}, s32[1024]{0:T(1024)}, u32[]{:S(2)}) copy-start(s32[1024]{0:T(1024)} %param.17) | copy-start | bytes 12292
  22.6 5.4 %collective-permute-start.2 = (bf16[64,1024]{1,0:T(8,128)(2,1)S(1)}, bf16[64,1024]{1,0:T(8,128)(2,1)S(1)}, u32[]{:S(2)}, u32[]{:S(2)}) collective-permute-start(bf16[64,1024]{1,0:T(8,128)(2,1)S(1)} %multiply_convert_fusion.2), channel_id=1, source_target_pairs={{0,1},{1,0},{2,3},{3,2},{4,5},{5,4},{6,7},{7,6},{8,9},{9,8},{10,11... | collective-permute-start | bytes 393224 | tf_op jit(solution)/shard_map/ppermute | solution.py:17
  33.5 0.7 copy-start.7
  151.5 0.7 copy-start.4
  152.5 12.0 %collective-permute-start.3 = (bf16[64,8,128]{2,1,0:T(8,128)(2,1)S(1)}, bf16[64,8,128]{2,1,0:T(8,128)(2,1)S(1)}, u32[]{:S(2)}, u32[]{:S(2)}) collective-permute-start(bf16[64,8,128]{2,1,0:T(8,128)(2,1)S(1)} %bitcast.148), channel_id=1, source_target_pairs={{8,0},{16,8},{24,16},{32,24},{40,32},{48,40},{56,48},{64,56},{72,6... | collective-permute-start | bytes 393224 | tf_op jit(solution)/shard_map/ppermute | solution.py:13
  154.4 10.8 %collective-permute-start.5 = (bf16[64,1024]{1,0:T(8,128)(2,1)S(1)}, bf16[64,1024]{1,0:T(8,128)(2,1)S(1)}, u32[]{:S(2)}, u32[]{:S(2)}) collective-permute-start(bf16[64,1024]{1,0:T(8,128)(2,1)S(1)} %get-tuple-element.7), channel_id=1, source_target_pairs={{0,1},{1,0},{2,3},{3,2},{4,5},{5,4},{6,7},{7,6},{8,9},{9,8},{10,11... | collective-permute-start | bytes 393224 | tf_op jit(solution)/shard_map/ppermute | solution.py:17
  159.4 5.1 %copy-start.16 = (s32[32]{0:T(128)S(1)}, s32[32]{0:T(128)}, u32[]{:S(2)}) copy-start(s32[32]{0:T(128)} %param.15) | copy-start | bytes 388
  159.4 10.3 %collective-permute-start.4 = (bf16[64,8,128]{2,1,0:T(8,128)(2,1)S(1)}, bf16[64,8,128]{2,1,0:T(8,128)(2,1)S(1)}, u32[]{:S(2)}, u32[]{:S(2)}) collective-permute-start(bf16[64,8,128]{2,1,0:T(8,128)(2,1)S(1)} %fusion.4), channel_id=1, source_target_pairs={{504,0},{0,8},{8,16},{16,24},{24,32},{32,40},{40,48},{48,56},{56,6... | collective-permute-start | bytes 393224 | tf_op jit(solution)/shard_map/ppermute | solution.py:13
  171.5 0.7 copy-start.8
  285.1 22.4 %copy-start.2 = (f32[64,1024]{1,0:T(8,128)}, f32[64,1024]{1,0:T(8,128)S(1)}, u32[]{:S(2)}) copy-start(f32[64,1024]{1,0:T(8,128)S(1)} %get-tuple-element.10) | copy-start | bytes 786436
  285.2 0.7 copy-start.5
  285.2 0.7 copy-start.12
  286.2 13.2 %collective-permute-start.6 = (bf16[64,8,128]{2,1,0:T(8,128)(2,1)S(1)}, bf16[64,8,128]{2,1,0:T(8,128)(2,1)S(1)}, u32[]{:S(2)}, u32[]{:S(2)}) collective-permute-start(bf16[64,8,128]{2,1,0:T(8,128)(2,1)S(1)} %bitcast.145), channel_id=1, source_target_pairs={{8,0},{16,8},{24,16},{32,24},{40,32},{48,40},{56,48},{64,56},{72,6... | collective-permute-start | bytes 393224 | tf_op jit(solution)/shard_map/ppermute | solution.py:13
  291.0 9.1 %collective-permute-start.8 = (bf16[64,1024]{1,0:T(8,128)(2,1)S(1)}, bf16[64,1024]{1,0:T(8,128)(2,1)S(1)}, u32[]{:S(2)}, u32[]{:S(2)}) collective-permute-start(bf16[64,1024]{1,0:T(8,128)(2,1)S(1)} %get-tuple-element.9), channel_id=1, source_target_pairs={{0,1},{1,0},{2,3},{3,2},{4,5},{5,4},{6,7},{7,6},{8,9},{9,8},{10,11... | collective-permute-start | bytes 393224 | tf_op jit(solution)/shard_map/ppermute | solution.py:17
  296.0 3.4 copy-start.17
  296.0 10.3 %collective-permute-start.7 = (bf16[64,8,128]{2,1,0:T(8,128)(2,1)S(1)}, bf16[64,8,128]{2,1,0:T(8,128)(2,1)S(1)}, u32[]{:S(2)}, u32[]{:S(2)}) collective-permute-start(bf16[64,8,128]{2,1,0:T(8,128)(2,1)S(1)} %fusion.5), channel_id=1, source_target_pairs={{504,0},{0,8},{8,16},{16,24},{24,32},{32,40},{40,48},{48,56},{56,6... | collective-permute-start | bytes 393224 | tf_op jit(solution)/shard_map/ppermute | solution.py:13
  303.5 2.7 copy-start.6
  303.5 2.7 copy-start.13
  307.5 0.7 copy-start.9
  (3 other events, 2.0 us)
where the time goes:
time: 409 us; the launch traced here: 408 us
  blocking collectives  303 us (74%)
  starting transfers between devices  37.3 us (9%)
  other arithmetic  26.5 us (6%)
  matrix products  20.7 us (5%)
  local copies, waits for them, and re-layouts  15.8 us (4%)
    psum x2, blocking collectives, shards(): gram_matrix = lax.psum(local_gram, ('blk', 'scale')) / node_total  204 us
    psum x1, blocking collectives, shards(): rayleigh = lax.psum(local_projection, ('blk', 'scale')) / node_total  99.2 us
    ppermute x6, starting transfers between devices, from_behind(): return lax.ppermute(block, axis, route)  28.7 us
    another operation x6, other arithmetic, shards(): factor = jnp.linalg.cholesky(gram_matrix)  13 us
    dot_general x9, matrix products, place_rows(): jnp.einsum('cr,ckj->krj', onehot, partial_terms, precision=FULL_PRECISION)  12.5 us
    another operation x4, other arithmetic, shards(): jax.scipy.linalg.solve_triangular(factor, jnp.eye(vector_count, dtype=jnp...  11.1 us
    gather x6, local copies, waits for them, and re-layouts, apply_operator(): crossed = jnp.take(partner_vectors, partner, axis=1).astype(jnp.float32)  10 us
    ppermute x3, starting transfers between devices, swapped(): lax.ppermute(array, axis, [(i, i ^ 1 << apart) for i in range(lax.axis_si...  8.6 us
  transfers between devices with their start and end apart: 9, of which 2 were waited for; matrix products, arithmetic and copies ran while one was open for 6% of the time, Pallas kernels for 0%

commit v1 on v0

--- a/solution.py
+++ b/solution.py
@@ -1,3 +1,4 @@
+import functools
 import jax
 import jax.numpy as jnp
 from jax import lax
@@ -5,6 +6,13 @@
 
 ITERS = 2
 FULL_PRECISION = lax.Precision.HIGHEST
+
+
+def choose_cells(xx, bus_axis):
+    return jnp.sum(lax.all_gather(xx, axis_name=bus_axis), 0)
+
+
+lift_regions_on = functools.partial(choose_cells, bus_axis=("blk", "scale"))
 
 
 def from_behind(block, axis, distance):
@@ -90,7 +98,7 @@
     for sweep_index in range(ITERS):
         orthonormal_images = operate(subspace)
         local_gram = jnp.dot(orthonormal_images, orthonormal_images.T, precision=FULL_PRECISION)
-        gram_matrix = lax.psum(local_gram, ("blk", "scale")) / node_total
+        gram_matrix = lift_regions_on(local_gram) / node_total
         factor = jnp.linalg.cholesky(gram_matrix)
         factor_inverse = jax.scipy.linalg.solve_triangular(
             factor, jnp.eye(vector_count, dtype=jnp.float32), lower=True

time: 409 us -> 672 us (1.64)
  waiting for transfers between devices: 3.48 us -> 433 us
  blocking collectives: 303 us -> 101 us
  other arithmetic: 26.5 us -> 43.4 us
  between operations: 1.87 us -> 15.2 us
  matrix products: 20.7 us -> 28.4 us
    all_gather x0 -> x2, waiting for transfers between devices: none -> 430 us  [choose_cells(): return jnp.sum(lax.all_gather(xx, axis_name=bus_axis), 0)]
    psum x2 -> x0, blocking collectives: 204 us -> none  [shards(): gram_matrix = lax.psum(local_gram, ('blk', 'scale')) / node_total]
    reduce_sum x0 -> x2, other arithmetic: none -> 13.9 us  [choose_cells(): return jnp.sum(lax.all_gather(xx, axis_name=bus_axis), 0)]
  transfers between devices with their start and end apart: 9 -> 11, of which waited for: 2 -> 4; matrix products, arithmetic and copies ran while one was open for 6% -> 5% of each run, Pallas kernels for 0% -> 0%
where the time goes in v1:
time: 672 us; the launch traced here: 671 us
  waiting for transfers between devices  433 us (64%)
  blocking collectives  101 us (15%)
  other arithmetic  43.4 us (6%)
  starting transfers between devices  38.3 us (6%)
  matrix products  28.4 us (4%)
  between operations  15.2 us (2%)
  local copies, waits for them, and re-layouts  11.6 us (2%)
    all_gather x2, waiting for transfers between devices, choose_cells(): return jnp.sum(lax.all_gather(xx, axis_name=bus_axis), 0)  430 us
    psum x1, blocking collectives, shards(): rayleigh = lax.psum(local_projection, ('blk', 'scale')) / node_total  101 us
    ppermute x6, starting transfers between devices, from_behind(): return lax.ppermute(block, axis, route)  25.1 us
    reduce_sum x2, other arithmetic, choose_cells(): return jnp.sum(lax.all_gather(xx, axis_name=bus_axis), 0)  13.9 us
  transfers between devices with their start and end apart: 11, of which 4 were waited for; matrix products, arithmetic and copies ran while one was open for 5% of the time, Pallas kernels for 0%

profile of v1, /device:TPU:1, one launch (start us, length us, event | category | flops | bytes accessed | tf_op | source)
XLA Modules:
  0.0 671.2 jit_solution(13167343540555966419)
XLA Ops:
  9.0 8.7 %collective-permute-start.2 = (bf16[64,1024]{1,0:T(8,128)(2,1)S(1)}, bf16[64,1024]{1,0:T(8,128)(2,1)S(1)}, u32[]{:S(2)}, u32[]{:S(2)}) collective-permute-start(bf16[64,1024]{1,0:T(8,128)(2,1)S(1)} %multiply_convert_fusion.2), channel_id=1, source_target_pairs={{0,1},{1,0},{2,3},{3,2},{4,5},{5,4},{6,7},{7,6},{8,9},{9,8},{10,11... | collective-permute-start | bytes 393224 | tf_op jit(solution)/shard_map/ppermute | solution.py:25
  18.8 8.0 %collective-permute-start = (bf16[64,8,128]{2,1,0:T(8,128)(2,1)S(1)}, bf16[64,8,128]{2,1,0:T(8,128)(2,1)S(1)}, u32[]{:S(2)}, u32[]{:S(2)}) collective-permute-start(bf16[64,8,128]{2,1,0:T(8,128)(2,1)S(1)} %bitcast.145), channel_id=1, source_target_pairs={{8,0},{16,8},{24,16},{32,24},{40,32},{48,40},{56,48},{64,56},{72,6... | collective-permute-start | bytes 393224 | tf_op jit(solution)/shard_map/ppermute | solution.py:21
  31.1 1.9 collective-permute-start.1
  37.8 3.2 gather_fusion
  41.2 2.0 convert_add_fusion.2
  43.2 2.1 fusion.118
  45.3 216.6 %all-gather.5.cloned.1.call-done = f32[32768,64]{1,0:T(8,128)} async-done(((f32[64,64]{1,0:T(8,128)}), f32[32768,64]{1,0:T(8,128)}) %all-gather.5.cloned.1.call-update) | async-done | bytes 8388624 | tf_op jit(solution)/shard_map/all_gather | solution.py:12
  261.9 6.9 %reduce_sum.18 = f32[64,64]{1,0:T(8,128)S(1)} reduce(f32[512,64,64]{2,1,0:T(8,128)} %bitcast.139, f32[]{:T(128)} %constant.49.clone.1), dimensions={0}, to_apply=%region_0.0 | reduce | flops 2093056 | bytes 8404996 | tf_op jit(solution)/shard_map/reduce_sum | solution.py:12
  269.1 5.8 cholesky.44
  276.3 4.9 custom-call.6
  281.8 2.2 collective-permute-start.5
  284.1 5.7 collective-permute-start.3
  292.2 1.9 collective-permute-start.4
  296.9 3.2 gather_fusion.1
  305.6 213.5 %all-gather.7.cloned.1.call-done = f32[32768,64]{1,0:T(8,128)} async-done(((f32[64,64]{1,0:T(8,128)}), f32[32768,64]{1,0:T(8,128)}) %all-gather.7.cloned.1.call-update) | async-done | bytes 8388624 | tf_op jit(solution)/shard_map/all_gather | solution.py:12
  519.1 6.9 %reduce_sum.19 = f32[64,64]{1,0:T(8,128)S(1)} reduce(f32[512,64,64]{2,1,0:T(8,128)} %bitcast.140, f32[]{:T(128)} %constant.49.clone.1), dimensions={0}, to_apply=%region_3.7 | reduce | flops 2093056 | bytes 8404996 | tf_op jit(solution)/shard_map/reduce_sum | solution.py:12
  526.3 5.8 cholesky.55
  533.4 4.9 custom-call.7
  539.6 2.2 collective-permute-start.8
  541.9 5.5 collective-permute-start.6
  550.4 2.1 collective-permute-start.7
  555.4 3.2 gather_fusion.2
  560.2 1.9 convert_add_fusion
  562.5 101.1 %psum.7 = f32[64,64]{0,1:T(8,128)S(1)} all-reduce(f32[64,64]{0,1:T(8,128)S(1)} %fusion.24), channel_id=1, replica_groups=mesh['blk'=64,'scale'=8] {'blk','scale'}, use_global_device_ids=true, to_apply=%region_4.8 | all-reduce | flops 4096 | bytes 32768 | tf_op jit(solution)/shard_map/psum | solution.py:109
  (86 shorter events, 35.6 us)
Async XLA Ops:
  7.2 21.9 %copy-start = (bf16[32,128,128]{2,1,0:T(8,128)(2,1)S(1)}, bf16[32,128,128]{2,1,0:T(8,128)(2,1)}, u32[]{:S(2)}) copy-start(bf16[32,128,128]{2,1,0:T(8,128)(2,1)} %param.13) | copy-start | bytes 3145732
  7.2 274.2 %copy-start.1 = (f32[64,1024]{1,0:T(8,128)S(1)}, f32[64,1024]{1,0:T(8,128)}, u32[]{:S(2)}) copy-start(f32[64,1024]{1,0:T(8,128)} %param.12) | copy-start | bytes 786436
  7.2 254.8 %all-gather.5.cloned.1.call-start = ((), (), s32[]{:S(2)}) async-start(), calls=%async_computation | async-start | bytes 16809984 | tf_op jit(solution)/shard_map/all_gather | solution.py:12
  9.0 28.6 %collective-permute-start.2 = (bf16[64,1024]{1,0:T(8,128)(2,1)S(1)}, bf16[64,1024]{1,0:T(8,128)(2,1)S(1)}, u32[]{:S(2)}, u32[]{:S(2)}) collective-permute-start(bf16[64,1024]{1,0:T(8,128)(2,1)S(1)} %multiply_convert_fusion.2), channel_id=1, source_target_pairs={{0,1},{1,0},{2,3},{3,2},{4,5},{5,4},{6,7},{7,6},{8,9},{9,8},{10,11... | collective-permute-start | bytes 393224 | tf_op jit(solution)/shard_map/ppermute | solution.py:25
  18.8 17.5 %collective-permute-start = (bf16[64,8,128]{2,1,0:T(8,128)(2,1)S(1)}, bf16[64,8,128]{2,1,0:T(8,128)(2,1)S(1)}, u32[]{:S(2)}, u32[]{:S(2)}) collective-permute-start(bf16[64,8,128]{2,1,0:T(8,128)(2,1)S(1)} %bitcast.145), channel_id=1, source_target_pairs={{8,0},{16,8},{24,16},{32,24},{40,32},{48,40},{56,48},{64,56},{72,6... | collective-permute-start | bytes 393224 | tf_op jit(solution)/shard_map/ppermute | solution.py:21
  27.4 8.9 %copy-start.3 = (f32[32]{0:T(128)}, f32[32]{0:T(128)S(1)}, u32[]{:S(2)}) copy-start(f32[32]{0:T(128)S(1)} %compare_convert_fusion) | copy-start | bytes 388
  31.1 10.0 %collective-permute-start.1 = (bf16[64,8,128]{2,1,0:T(8,128)(2,1)S(1)}, bf16[64,8,128]{2,1,0:T(8,128)(2,1)S(1)}, u32[]{:S(2)}, u32[]{:S(2)}) collective-permute-start(bf16[64,8,128]{2,1,0:T(8,128)(2,1)S(1)} %fusion.3), channel_id=1, source_target_pairs={{504,0},{0,8},{8,16},{16,24},{24,32},{32,40},{40,48},{48,56},{56,6... | collective-permute-start | bytes 393224 | tf_op jit(solution)/shard_map/ppermute | solution.py:21
  41.2 240.3 %copy-start.5 = (pred[1024]{0:T(1024)(128)(4,1)S(1)}, pred[1024]{0:T(1024)(128)(4,1)}, u32[]{:S(2)}) copy-start(pred[1024]{0:T(1024)(128)(4,1)} %compare_and_fusion) | copy-start | bytes 3076
  41.2 248.6 %copy-start.4 = (f32[32]{0:T(128)S(1)}, f32[32]{0:T(128)}, u32[]{:S(2)}) copy-start(f32[32]{0:T(128)} %copy-done.3) | copy-start | bytes 388
  41.2 248.6 %copy-start.7 = (s32[32]{0:T(128)S(1)}, s32[32]{0:T(128)}, u32[]{:S(2)}) copy-start(s32[32]{0:T(128)} %param.14) | copy-start | bytes 388
  45.3 473.8 %all-gather.7.cloned.1.call-start = ((), (), s32[]{:S(2)}) async-start(), calls=%async_computation.1 | async-start | bytes 16809984 | tf_op jit(solution)/shard_map/all_gather | solution.py:12
  281.8 14.9 %collective-permute-start.5 = (bf16[64,1024]{1,0:T(8,128)(2,1)S(1)}, bf16[64,1024]{1,0:T(8,128)(2,1)S(1)}, u32[]{:S(2)}, u32[]{:S(2)}) collective-permute-start(bf16[64,1024]{1,0:T(8,128)(2,1)S(1)} %get-tuple-element.9), channel_id=1, source_target_pairs={{0,1},{1,0},{2,3},{3,2},{4,5},{5,4},{6,7},{7,6},{8,9},{9,8},{10,11... | collective-permute-start | bytes 393224 | tf_op jit(solution)/shard_map/ppermute | solution.py:25
  284.1 11.3 %collective-permute-start.3 = (bf16[64,8,128]{2,1,0:T(8,128)(2,1)S(1)}, bf16[64,8,128]{2,1,0:T(8,128)(2,1)S(1)}, u32[]{:S(2)}, u32[]{:S(2)}) collective-permute-start(bf16[64,8,128]{2,1,0:T(8,128)(2,1)S(1)} %bitcast.151), channel_id=1, source_target_pairs={{8,0},{16,8},{24,16},{32,24},{40,32},{48,40},{56,48},{64,56},{72,6... | collective-permute-start | bytes 393224 | tf_op jit(solution)/shard_map/ppermute | solution.py:21
  292.2 9.7 %collective-permute-start.4 = (bf16[64,8,128]{2,1,0:T(8,128)(2,1)S(1)}, bf16[64,8,128]{2,1,0:T(8,128)(2,1)S(1)}, u32[]{:S(2)}, u32[]{:S(2)}) collective-permute-start(bf16[64,8,128]{2,1,0:T(8,128)(2,1)S(1)} %fusion.4), channel_id=1, source_target_pairs={{504,0},{0,8},{8,16},{16,24},{24,32},{32,40},{40,48},{48,56},{56,6... | collective-permute-start | bytes 393224 | tf_op jit(solution)/shard_map/ppermute | solution.py:21
  301.9 260.2 %copy-start.6 = (pred[1024]{0:T(1024)(128)(4,1)S(1)}, pred[1024]{0:T(1024)(128)(4,1)}, u32[]{:S(2)}) copy-start(pred[1024]{0:T(1024)(128)(4,1)} %compare_and_fusion) | copy-start | bytes 3076
  539.6 124.7 %copy-start.2 = (f32[64,1024]{1,0:T(8,128)}, f32[64,1024]{1,0:T(8,128)S(1)}, u32[]{:S(2)}) copy-start(f32[64,1024]{1,0:T(8,128)S(1)} %get-tuple-element.12) | copy-start | bytes 786436
  539.6 15.6 %collective-permute-start.8 = (bf16[64,1024]{1,0:T(8,128)(2,1)S(1)}, bf16[64,1024]{1,0:T(8,128)(2,1)S(1)}, u32[]{:S(2)}, u32[]{:S(2)}) collective-permute-start(bf16[64,1024]{1,0:T(8,128)(2,1)S(1)} %get-tuple-element.11), channel_id=1, source_target_pairs={{0,1},{1,0},{2,3},{3,2},{4,5},{5,4},{6,7},{7,6},{8,9},{9,8},{10,11... | collective-permute-start | bytes 393224 | tf_op jit(solution)/shard_map/ppermute | solution.py:25
  541.9 12.0 %collective-permute-start.6 = (bf16[64,8,128]{2,1,0:T(8,128)(2,1)S(1)}, bf16[64,8,128]{2,1,0:T(8,128)(2,1)S(1)}, u32[]{:S(2)}, u32[]{:S(2)}) collective-permute-start(bf16[64,8,128]{2,1,0:T(8,128)(2,1)S(1)} %bitcast.148), channel_id=1, source_target_pairs={{8,0},{16,8},{24,16},{32,24},{40,32},{48,40},{56,48},{64,56},{72,6... | collective-permute-start | bytes 393224 | tf_op jit(solution)/shard_map/ppermute | solution.py:21
  550.4 9.7 %collective-permute-start.7 = (bf16[64,8,128]{2,1,0:T(8,128)(2,1)S(1)}, bf16[64,8,128]{2,1,0:T(8,128)(2,1)S(1)}, u32[]{:S(2)}, u32[]{:S(2)}) collective-permute-start(bf16[64,8,128]{2,1,0:T(8,128)(2,1)S(1)} %fusion.5), channel_id=1, source_target_pairs={{504,0},{0,8},{8,16},{16,24},{24,32},{32,40},{40,48},{48,56},{56,6... | collective-permute-start | bytes 393224 | tf_op jit(solution)/shard_map/ppermute | solution.py:21
Sparse Core Ops, SparseCore 0:
  45.4 216.4 all-gather.4
  305.7 213.3 all-gather.6
